TPU v7x, 32 devices: a whole 2x2x4 slice. The times are simulated.
32 devices in a mesh: lat: 2 (over y), lon: 16 (over z, x, core).
Axes of the slice: x: 2, y: 2, z: 4, core: 2. Of those that a mesh axis runs over, the one named last changes fastest.
Arguments:
- sea_level: float32 [2048, 256], P('lon', 'lat'), may hold values from -1 to 5
- east_velocity: float32 [2048, 256], P('lon', 'lat'), may hold values from -6 to 6
- north_velocity: float32 [2048, 256], P('lon', 'lat'), may hold values from -6 to 6
- depth: float32 [2048, 256], P('lon', 'lat'), may hold values from 0.25 to 1
- land_mask: int32 [2048, 256], P('lon', 'lat'), may hold values from 0 to 1, as said below
- wet_counts: int32 [2, 16], replicated, may hold values from 1 to 16384, as said below
- loading_prev: float32 [2048, 256], P('lon', 'lat'), may hold values from -4 to 4
- tide_amp: float32 [8], replicated, may hold values from 0.3 to 1
- tide_phase: float32 [8], replicated, may hold values from -3.140625 to 3.140625
- legendre: bfloat16 [512, 1024, 256], P('lon', None, 'lat'), may hold values from -0.375 to 0.375
- love_factor: float32 [1024], replicated, may hold values from 0.05 to 1
Outputs:
- height_new: float32 [2048, 256], P('lon', 'lat')
- east_new: float32 [2048, 256], P('lon', 'lat')
- north_new: float32 [2048, 256], P('lon', 'lat')
- self_attraction: float32 [2048, 256], P('lon', 'lat')
Inputs may be any that keep to these rules, and one draw needn't show every extreme that they name: `land_mask`: every tile of 128 columns by 128 rows holds at least one wet column, and one tile is wholly wet. wet_counts[p, q] is the number of wet columns of land_mask in latitude band p and longitude band q.
All inputs are finite; a program needn't handle non-finite values.
Results may differ from a plain program's by a relative error of at most 0.0038.
Values may be sent and summed in bfloat16 or wider, within the bound.
No kernel may reach another device: no remote copies, remote signals or barrier semaphores. Data moves between devices by JAX's collectives and lax.ppermute only.
A program may use at most 64 MiB of HBM per device.

v0:
```python
import math
import jax
import jax.numpy as jnp
from jax import lax
from jax.sharding import PartitionSpec as P

SUBSTEPS = 4
lat_edge = 1.3089969
courant = 0.4
friction = 0.02
rotation = 0.2
frequencies = (0.1405, 0.1454, 0.1379, 0.1458, 0.0729, 0.0676, 0.0725, 0.0649)
orders = (2, 2, 2, 2, 1, 1, 1, 1)
highest = lax.Precision.HIGHEST


def padded(cells, sides, width, closed):
    for axis, dim in sides:
        count = lax.axis_size(axis)
        ends = count if closed else count - 1
        head = lax.slice_in_dim(cells, 0, width, axis=dim)
        tail = lax.slice_in_dim(cells, cells.shape[dim] - width, cells.shape[dim], axis=dim)
        cells = jnp.concatenate(
            [
                lax.ppermute(tail, axis, [(i, (i + 1) % count) for i in range(ends)]),
                cells,
                lax.ppermute(head, axis, [((i + 1) % count, i) for i in range(ends)]),
            ],
            axis=dim,
        )
    return cells


def latitude_of(rows, total_rows):
    return -lat_edge + 2.0 * lat_edge * (rows.astype(jnp.float32) + 0.5) / total_rows


def potential(columns, rows, moment, total_cols, total_rows, tide_amp, tide_phase):
    longitude = (2.0 * math.pi * (columns % total_cols).astype(jnp.float32) / total_cols)[:, None]
    latitude = latitude_of(rows, total_rows)[None, :]
    semi = jnp.cos(latitude) ** 2
    diurnal = jnp.sin(2.0 * latitude)
    field = jnp.zeros((columns.shape[0], rows.shape[0]), jnp.float32)
    for index in range(len(frequencies)):
        shape_term = semi if orders[index] == 2 else diurnal
        field = field + tide_amp[index] * shape_term * jnp.cos(
            frequencies[index] * moment + orders[index] * longitude + tide_phase[index]
        )
    return field * (total_cols / 64.0)


def advance(state_x, static_x, forcing, latitude_x):
    height_x, east_x, north_x = (state_x[0], state_x[1], state_x[2])
    depth_x, wet_x, loading_x = (static_x[0], static_x[1], static_x[2])
    cosine = jnp.cos(latitude_x)[None, :]
    secant_cycle = (1.0 / jnp.cos(latitude_x[1:-1]))[None, :]
    secant_core = (1.0 / jnp.cos(latitude_x[2:-2]))[None, :]
    coriolis = (rotation * jnp.sin(latitude_x[2:-2]))[None, :]
    flux_east = depth_x * east_x
    flux_north = depth_x * north_x * cosine
    divergence = (
        (
            flux_east[2:, 1:-1]
            - flux_east[:-2, 1:-1]
            + (flux_north[1:-1, 2:] - flux_north[1:-1, :-2])
        )
        * 0.5
        * secant_cycle
    )
    height_cycle = height_x[1:-1, 1:-1] - courant * divergence * wet_x[1:-1, 1:-1]
    pressure = height_cycle - forcing - loading_x[1:-1, 1:-1]
    slope_east = (pressure[2:, 1:-1] - pressure[:-2, 1:-1]) * 0.5 * secant_core
    slope_north = (pressure[1:-1, 2:] - pressure[1:-1, :-2]) * 0.5
    east = east_x[2:-2, 2:-2]
    north = north_x[2:-2, 2:-2]
    wet = wet_x[2:-2, 2:-2]
    east_next = wet * ((1.0 - friction) * east + courant * (coriolis * north - slope_east))
    north_next = wet * ((1.0 - friction) * north - courant * (coriolis * east + slope_north))
    return jnp.stack([height_cycle[1:-1, 1:-1], east_next, north_next])


def extend_margin(fields, margin):
    wide = padded(fields, (("lon", 1),), margin, True)
    return padded(wide, (("lat", 2),), margin, False)


def wave_table(waves, columns, total_cols, weights):
    turns = waves[None, :] * columns[:, None] % total_cols
    angle = 2.0 * math.pi * turns.astype(jnp.float32) / total_cols
    scale = weights[None, :] / math.sqrt(total_cols)
    return jnp.stack([scale * jnp.cos(angle), -scale * jnp.sin(angle)], axis=2)


def shards(
    sea_level,
    east_velocity,
    north_velocity,
    depth,
    land_mask,
    wet_counts,
    loading_prev,
    tide_amp,
    tide_phase,
    legendre,
    love_factor,
):
    lon_dev, lat_dev = sea_level.shape
    wave_dev = legendre.shape[0]
    lon_count = lax.axis_size("lon")
    total_cols = lon_dev * lon_count
    total_rows = lat_dev * lax.axis_size("lat")
    lon_index = lax.axis_index("lon")
    lon_start = lon_index * lon_dev
    lat_start = lax.axis_index("lat") * lat_dev
    wet = land_mask.astype(jnp.float32)
    margin = 2 * SUBSTEPS
    full = extend_margin(
        jnp.stack([sea_level, east_velocity, north_velocity, depth, wet, loading_prev]), margin
    )
    state_x = full[:3]
    static_full = full[3:]
    wide_cols = full.shape[1]
    wide_rows = full.shape[2]
    for moment in range(SUBSTEPS):
        reach = margin - 2 * moment
        offset = margin - reach
        static_x = static_full[:, offset : wide_cols - offset, offset : wide_rows - offset]
        latitude_x = jnp.clip(
            latitude_of(
                lat_start + jnp.arange(-reach, lat_dev + reach, dtype=jnp.int32), total_rows
            ),
            -1.5,
            1.5,
        )
        columns = lon_start + jnp.arange(1 - reach, lon_dev + reach - 1, dtype=jnp.int32)
        rows = lat_start + jnp.arange(1 - reach, lat_dev + reach - 1, dtype=jnp.int32)
        forcing = potential(
            columns, rows, float(moment), total_cols, total_rows, tide_amp, tide_phase
        )
        state_x = advance(state_x, static_x, forcing, latitude_x)
    height = state_x[0]
    wet_sum = lax.psum(jnp.sum(wet * height), ("lat", "lon"))
    mean_level = wet_sum / jnp.sum(wet_counts.astype(jnp.float32))
    anomaly = wet * (height - mean_level)
    local_cols = lon_start + jnp.arange(lon_dev, dtype=jnp.int32)
    count = wave_dev * lax.axis_size("lon")
    waves = jnp.arange(count, dtype=jnp.int32)
    table = wave_table(waves, local_cols, total_cols, jnp.ones((count,), jnp.float32))
    table = jnp.transpose(table, (1, 2, 0)).reshape(2 * count, lon_dev)
    fourier = lax.psum_scatter(
        jnp.dot(table, anomaly, precision=highest, preferred_element_type=jnp.float32).reshape(
            count, 2, lat_dev
        ),
        "lon",
        scatter_dimension=0,
        tiled=True,
    ).astype(jnp.bfloat16)
    coefficients = lax.dot_general(
        fourier, legendre, (((2,), (2,)), ((0,), (0,))), preferred_element_type=jnp.float32
    )
    coefficients = lax.psum(coefficients, "lat")
    scaled = (coefficients * love_factor[None, None, :]).astype(jnp.bfloat16)
    synthesis = lax.dot_general(
        scaled, legendre, (((2,), (1,)), ((0,), (0,))), preferred_element_type=jnp.float32
    )
    own_waves = lon_index * wave_dev + jnp.arange(wave_dev, dtype=jnp.int32)
    weights = jnp.where(own_waves == 0, 1.0, 2.0).astype(jnp.float32)
    flat_spectra = synthesis.reshape(2 * wave_dev, lat_dev)
    count = lon_dev * lax.axis_size("lon")
    cells = jnp.arange(count, dtype=jnp.int32)
    table = wave_table(own_waves, cells, total_cols, weights).reshape(count, 2 * wave_dev)
    self_attraction = lax.psum_scatter(
        jnp.dot(table, flat_spectra, precision=highest, preferred_element_type=jnp.float32),
        "lon",
        scatter_dimension=0,
        tiled=True,
    )
    return (state_x[0], state_x[1], state_x[2], self_attraction)


def solution(mesh):
    placed = (
        P("lon", "lat"),
        P("lon", "lat"),
        P("lon", "lat"),
        P("lon", "lat"),
        P("lon", "lat"),
        P(),
        P("lon", "lat"),
        P(),
        P(),
        P("lon", None, "lat"),
        P(),
    )
    return jax.shard_map(
        shards,
        mesh=mesh,
        in_specs=placed,
        out_specs=(P("lon", "lat"), P("lon", "lat"), P("lon", "lat"), P("lon", "lat")),
        check_vma=False,
    )
```

profile of v0, /device:TPU:0, one launch (start us, length us, event | category | flops | bytes accessed | tf_op | source)
XLA Modules:
  0.0 292.7 jit_solution(6166529491891947540)
XLA Ops:
  7.2 0.8 bitcast_dynamic-update-slice_fusion.5
  8.1 0.8 bitcast_dynamic-update-slice_fusion.4
  8.9 0.8 bitcast_dynamic-update-slice_fusion.3
  9.7 0.8 bitcast_dynamic-update-slice_fusion.2
  10.6 0.8 bitcast_dynamic-update-slice_fusion.1
  11.4 0.8 bitcast_dynamic-update-slice_fusion
  12.3 0.5 collective-permute-start
  12.8 5.0 %collective-permute-start.1 = (f32[6,8,128]{2,1,0:T(8,128)S(1)}, f32[6,8,128]{2,1,0:T(8,128)S(1)}, u32[]{:S(2)}, u32[]{:S(2)}) collective-permute-start(f32[6,8,128]{2,1,0:T(8,128)S(1)} %get-tuple-element.50), channel_id=1, source_target_pairs={{1,0},{2,1},{3,2},{4,3},{5,4},{6,5},{7,6},{8,7},{9,8},{10,9},{11,1... | collective-permute-start | bytes 73736 | tf_op jit(solution)/shard_map/ppermute | solution.py:27
  18.2 1.6 fusion.116
  19.8 1.2 broadcast_multiply_fusion.30
  21.1 1.2 broadcast_multiply_fusion.20
  22.3 1.3 broadcast_multiply_fusion.32
  23.6 1.3 broadcast_multiply_fusion.22
  24.9 1.3 broadcast_multiply_fusion.35
  26.2 1.3 broadcast_multiply_fusion.25
  27.5 1.2 broadcast_multiply_fusion.37
  28.7 1.2 broadcast_multiply_fusion.27
  30.0 1.6 fusion.117
  31.6 1.4 add_cosine_fusion.28
  33.0 1.4 add_cosine_fusion.20
  34.4 1.3 add_cosine_fusion.30
  35.7 1.3 add_cosine_fusion.22
  37.0 1.4 add_cosine_fusion.24
  38.4 1.4 add_cosine_fusion.16
  39.8 1.4 add_cosine_fusion.26
  41.1 1.4 add_cosine_fusion.18
  42.8 1.2 broadcast_multiply_fusion.10
  44.0 1.3 broadcast_multiply_fusion.12
  45.3 1.3 broadcast_multiply_fusion.15
  46.6 1.2 broadcast_multiply_fusion.17
  47.9 1.4 add_cosine_fusion.8
  49.2 1.4 add_cosine_fusion.10
  50.6 1.4 add_cosine_fusion.12
  52.0 1.3 add_cosine_fusion.14
  53.6 1.2 broadcast_multiply_fusion
  54.9 1.3 broadcast_multiply_fusion.2
  56.1 1.3 broadcast_multiply_fusion.5
  57.4 1.2 broadcast_multiply_fusion.7
  58.7 1.4 add_cosine_fusion
  60.1 1.4 add_cosine_fusion.2
  61.4 1.4 add_cosine_fusion.4
  62.8 1.3 add_cosine_fusion.6
  64.3 1.3 convert_reduce_fusion
  65.6 1.1 cosine_multiply_fusion
  66.9 4.0 %collective-permute-start.2 = (f32[6,144,8]{2,1,0:T(8,128)S(1)}, f32[6,144,8]{2,1,0:T(8,128)S(1)}, u32[]{:S(2)}, u32[]{:S(2)}) collective-permute-start(f32[6,144,8]{2,1,0:T(8,128)S(1)} %get-tuple-element.47), channel_id=1, source_target_pairs={{0,16},{1,17},{2,18},{3,19},{4,20},{5,21},{6,22},{7,23},{8,24},{9,... | collective-permute-start | bytes 82952 | tf_op jit(solution)/shard_map/ppermute | solution.py:25
  70.9 1.3 collective-permute-start.3
  72.3 1.2 dynamic-slice
  74.2 3.5 %collective-permute-done.2 = f32[6,144,8]{2,1,0:T(8,128)S(1)} collective-permute-done((f32[6,144,8]{2,1,0:T(8,128)S(1)}, f32[6,144,8]{2,1,0:T(8,128)S(1)}, u32[]{:S(2)}, u32[]{:S(2)}) %collective-permute-start.2) | collective-permute-done | bytes 27680 | tf_op jit(solution)/shard_map/ppermute | solution.py:25
  77.7 4.1 %collective-permute-done.3 = f32[6,144,8]{2,1,0:T(8,128)S(1)} collective-permute-done((f32[6,144,8]{2,1,0:T(8,128)S(1)}, f32[6,144,8]{2,1,0:T(8,128)S(1)}, u32[]{:S(2)}, u32[]{:S(2)}) %collective-permute-start.3) | collective-permute-done | bytes 27680 | tf_op jit(solution)/shard_map/ppermute | solution.py:27
  82.7 0.5 slice_subtract_fusion.5
  83.6 0.5 slice_subtract_fusion
  84.4 0.4 slice_subtract_fusion.13
  85.2 0.4 slice_subtract_fusion.8
  85.6 0.7 multiply_reduce_fusion
  86.3 39.7 %psum.14 = f32[]{:T(128)} all-reduce(f32[]{:T(128)} %get-tuple-element.4), channel_id=1, replica_groups=mesh['lat'=2,'lon'=16] {'lat','lon'}, use_global_device_ids=true, to_apply=%region_1.2 | all-reduce | flops 1 | bytes 8 | tf_op jit(solution)/shard_map/psum | solution.py:142
  127.4 1.0 fusion.3
  128.8 65.7 %all-reduce.5 = bf16[512,2,128]{2,1,0:T(2,128)(2,1)S(1)} all-reduce(f32[512,2,128]{2,1,0:T(2,128)S(1)} %copy.15), channel_id=2, replica_groups=mesh['lat'=2,'lon'=16] {'lon'}, use_global_device_ids=true, to_apply=%region_3.4.clone | all-reduce | flops 131072 | bytes 786432
  194.5 6.4 %fusion.86 = f32[32,2,1024]{2,1,0:T(2,128)} fusion(bf16[32,1024,128]{2,1,0:T(8,128)(2,1)} %param.20, bf16[512,2,128]{2,1,0:T(2,128)(2,1)S(1)} %all-reduce.5, u32[]{:T(128)S(6)} %multiply.402), kind=kOutput, calls=%fused_computation.152 | convolution fusion | flops 16777216 | bytes 8667140 | tf_op jit(solution)/shard_map/dot_general | solution.py:158
  201.1 1.1 cosine_multiply_fusion.1
  202.2 18.4 %all-reduce.4.cloned.1.call-done = f32[32,2,1024]{2,1,0:T(2,128)} async-done(((f32[32,2,1024]{2,1,0:T(2,128)}), f32[32,2,1024]{2,1,0:T(2,128)}) %all-reduce.4.cloned.1.call-update) | async-done | bytes 262160 | tf_op jit(solution)/shard_map/psum | solution.py:161
  220.6 4.7 %fusion.66 = f32[32,2,128]{2,1,0:T(2,128)S(1)} fusion(bf16[32,1024,128]{2,1,0:T(8,128)(2,1)} %param.20, f32[32,2,1024]{2,1,0:T(2,128)} %all-reduce.4.cloned.1.call-done, f32[1024]{0:T(1024)S(1)} %copy-done.2), kind=kOutput, calls=%fused_computation.122 | convolution fusion | flops 16908288 | bytes 8687616 | tf_op jit(solution)/shard_map/dot_general | solution.py:163
  225.3 2.8 convolution_bitcast_fusion
  228.2 0.8 fusion.74
  229.1 56.8 %reduce-scatter.2.cloned.1.call-done = f32[128,128]{1,0:T(8,128)} async-done(((f32[2048,128]{1,0:T(8,128)}), f32[128,128]{1,0:T(8,128)}) %reduce-scatter.2.cloned.1.call-update) | async-done | bytes 65552 | tf_op jit(solution)/shard_map/reduce_scatter | solution.py:172
  (40 shorter events, 4.0 us)
Async XLA Ops:
  7.2 213.4 %all-reduce.4.cloned.1.call-start = ((), (), s32[]{:S(2)}) async-start(), calls=%async_computation.1 | async-start | bytes 524288 | tf_op jit(solution)/shard_map/psum | solution.py:161
  12.3 54.4 %collective-permute-start = (f32[6,8,128]{2,1,0:T(8,128)S(1)}, f32[6,8,128]{2,1,0:T(8,128)S(1)}, u32[]{:S(2)}, u32[]{:S(2)}) collective-permute-start(f32[6,8,128]{2,1,0:T(8,128)S(1)} %get-tuple-element.49), channel_id=1, source_target_pairs={{0,1},{1,2},{2,3},{3,4},{4,5},{5,6},{6,7},{7,8},{8,9},{9,10},{10,1... | collective-permute-start | bytes 73736 | tf_op jit(solution)/shard_map/ppermute | solution.py:25
  12.8 53.9 %collective-permute-start.1 = (f32[6,8,128]{2,1,0:T(8,128)S(1)}, f32[6,8,128]{2,1,0:T(8,128)S(1)}, u32[]{:S(2)}, u32[]{:S(2)}) collective-permute-start(f32[6,8,128]{2,1,0:T(8,128)S(1)} %get-tuple-element.50), channel_id=1, source_target_pairs={{1,0},{2,1},{3,2},{4,3},{5,4},{6,5},{7,6},{8,7},{9,8},{10,9},{11,1... | collective-permute-start | bytes 73736 | tf_op jit(solution)/shard_map/ppermute | solution.py:27
  66.9 18.7 %copy-start = (s32[128,128]{1,0:T(8,128)S(1)}, s32[128,128]{1,0:T(8,128)}, u32[]{:S(2)}) copy-start(s32[128,128]{1,0:T(8,128)} %param.15) | copy-start | bytes 196612
  66.9 10.7 %collective-permute-start.2 = (f32[6,144,8]{2,1,0:T(8,128)S(1)}, f32[6,144,8]{2,1,0:T(8,128)S(1)}, u32[]{:S(2)}, u32[]{:S(2)}) collective-permute-start(f32[6,144,8]{2,1,0:T(8,128)S(1)} %get-tuple-element.47), channel_id=1, source_target_pairs={{0,16},{1,17},{2,18},{3,19},{4,20},{5,21},{6,22},{7,23},{8,24},{9,... | collective-permute-start | bytes 82952 | tf_op jit(solution)/shard_map/ppermute | solution.py:25
  70.9 10.9 %collective-permute-start.3 = (f32[6,144,8]{2,1,0:T(8,128)S(1)}, f32[6,144,8]{2,1,0:T(8,128)S(1)}, u32[]{:S(2)}, u32[]{:S(2)}) collective-permute-start(f32[6,144,8]{2,1,0:T(8,128)S(1)} %get-tuple-element.48), channel_id=1, source_target_pairs={{16,0},{17,1},{18,2},{19,3},{20,4},{21,5},{22,6},{23,7},{24,8},{25... | collective-permute-start | bytes 82952 | tf_op jit(solution)/shard_map/ppermute | solution.py:27
  84.4 136.2 %copy-start.2 = (f32[1024]{0:T(1024)S(1)}, f32[1024]{0:T(1024)}, u32[]{:S(2)}) copy-start(f32[1024]{0:T(1024)} %param.21) | copy-start | bytes 12292
  86.3 138.9 %copy-start.1 = (f32[128,128]{1,0:T(8,128)}, f32[128,128]{1,0:T(8,128)S(1)}, u32[]{:S(2)}) copy-start(f32[128,128]{1,0:T(8,128)S(1)} %get-tuple-element.5) | copy-start | bytes 196612
  200.9 85.0 %reduce-scatter.2.cloned.1.call-start = ((), (), s32[]{:S(2)}) async-start(), calls=%async_computation.2 | async-start | bytes 1114112 | tf_op jit(solution)/shard_map/reduce_scatter | solution.py:172
Sparse Core Ops, SparseCore 0:
  201.0 19.5 all-reduce.3
  228.2 57.5 reduce-scatter.1
where the time goes:
time: 294 us; the launch traced here: 293 us
  blocking collectives  105 us (36%)
  waiting for transfers between devices  82.9 us (28%)
  other arithmetic  52.3 us (18%)
  between operations  16.4 us (6%)
  matrix products  14.9 us (5%)
  starting transfers between devices  11.1 us (4%)
  local copies, waits for them, and re-layouts  9.8 us (3%)
    unnamed x1, blocking collectives  65.7 us
    reduce_scatter x1, waiting for transfers between devices, shards(): lax.psum_scatter(jnp.dot(table, flat_spectra, precision=highest, preferre...  56.8 us
    psum x1, blocking collectives, shards(): wet_sum = lax.psum(jnp.sum(wet * height), ('lat', 'lon'))  39.7 us
    cos x16, other arithmetic, potential(): jnp.cos(frequencies[index] * moment + orders[index] * longitude + tide_ph...  21.7 us
    mul x16, other arithmetic, potential(): tide_amp[index] * shape_term  20.3 us
    psum x1, waiting for transfers between devices, shards(): coefficients = lax.psum(coefficients, 'lat')  18.4 us
    dot_general x1, matrix products, shards(): lax.dot_general(fourier, legendre, (((2,), (2,)), ((0,), (0,))), preferre...  6.37 us
    ppermute x2, starting transfers between devices, padded(): lax.ppermute(head, axis, [((i + 1) % count, i) for i in range(ends)])  6.31 us
  transfers between devices with their start and end apart: 6, of which 4 were waited for; matrix products, arithmetic and copies ran while one was open for 18% of the time, Pallas kernels for 0%

commit v1 on v0

--- a/solution.py
+++ b/solution.py
@@ -12,6 +12,12 @@
 frequencies = (0.1405, 0.1454, 0.1379, 0.1458, 0.0729, 0.0676, 0.0725, 0.0649)
 orders = (2, 2, 2, 2, 1, 1, 1, 1)
 highest = lax.Precision.HIGHEST
+
+
+def summed_here(value, mesh_axis):
+    parts = lax.all_gather(value, mesh_axis, axis=0, tiled=False)
+    total = parts.sum(axis=0)
+    return total
 
 
 def padded(cells, sides, width, closed):
@@ -158,7 +164,7 @@
     coefficients = lax.dot_general(
         fourier, legendre, (((2,), (2,)), ((0,), (0,))), preferred_element_type=jnp.float32
     )
-    coefficients = lax.psum(coefficients, "lat")
+    coefficients = summed_here(coefficients, "lat")
     scaled = (coefficients * love_factor[None, None, :]).astype(jnp.bfloat16)
     synthesis = lax.dot_general(
         scaled, legendre, (((2,), (1,)), ((0,), (0,))), preferred_element_type=jnp.float32

time: 294 us -> 280 us (0.952)
  waiting for transfers between devices: 82.9 us -> 61.2 us
  blocking collectives: 105 us -> 113 us
    psum x1 -> x0, waiting for transfers between devices: 18.4 us -> none  [shards(): coefficients = lax.psum(coefficients, 'lat')]
    all_gather x0 -> x1, blocking collectives: none -> 7.03 us  [summed_here(): parts = lax.all_gather(value, mesh_axis, axis=0, tiled=False)]
  transfers between devices with their start and end apart: 6 -> 5, of which waited for: 4 -> 3; matrix products, arithmetic and copies ran while one was open for 18% -> 19% of each run, Pallas kernels for 0% -> 0%
where the time goes in v1:
time: 280 us; the launch traced here: 279 us
  blocking collectives  113 us (40%)
  waiting for transfers between devices  61.2 us (22%)
  other arithmetic  54 us (19%)
  between operations  16.4 us (6%)
  matrix products  14.1 us (5%)
  starting transfers between devices  10.9 us (4%)
  local copies, waits for them, and re-layouts  9.8 us (4%)
    unnamed x1, blocking collectives  65.9 us
    reduce_scatter x1, waiting for transfers between devices, shards(): lax.psum_scatter(jnp.dot(table, flat_spectra, precision=highest, preferre...  54.8 us
    psum x1, blocking collectives, shards(): wet_sum = lax.psum(jnp.sum(wet * height), ('lat', 'lon'))  39.7 us
    cos x16, other arithmetic, potential(): jnp.cos(frequencies[index] * moment + orders[index] * longitude + tide_ph...  21.2 us
    mul x16, other arithmetic, potential(): tide_amp[index] * shape_term  21.2 us
    all_gather x1, blocking collectives, summed_here(): parts = lax.all_gather(value, mesh_axis, axis=0, tiled=False)  7.03 us
    ppermute x2, starting transfers between devices, padded(): lax.ppermute(head, axis, [((i + 1) % count, i) for i in range(ends)])  6.31 us
    dot_general x1, matrix products, shards(): lax.dot_general(fourier, legendre, (((2,), (2,)), ((0,), (0,))), preferre...  5.66 us
  transfers between devices with their start and end apart: 5, of which 3 were waited for; matrix products, arithmetic and copies ran while one was open for 19% of the time, Pallas kernels for 0%

profile of v1, /device:TPU:0, one launch (start us, length us, event | category | flops | bytes accessed | tf_op | source)
XLA Modules:
  0.0 279.0 jit_solution(10400572264948385921)
XLA Ops:
  7.2 0.8 bitcast_dynamic-update-slice_fusion.5
  8.1 0.8 bitcast_dynamic-update-slice_fusion.4
  8.9 0.8 bitcast_dynamic-update-slice_fusion.3
  9.7 0.8 bitcast_dynamic-update-slice_fusion.2
  10.6 0.8 bitcast_dynamic-update-slice_fusion.1
  11.4 0.8 bitcast_dynamic-update-slice_fusion
  12.3 0.5 collective-permute-start
  12.8 5.0 %collective-permute-start.1 = (f32[6,8,128]{2,1,0:T(8,128)S(1)}, f32[6,8,128]{2,1,0:T(8,128)S(1)}, u32[]{:S(2)}, u32[]{:S(2)}) collective-permute-start(f32[6,8,128]{2,1,0:T(8,128)S(1)} %get-tuple-element.50), channel_id=1, source_target_pairs={{1,0},{2,1},{3,2},{4,3},{5,4},{6,5},{7,6},{8,7},{9,8},{10,9},{11,1... | collective-permute-start | bytes 73736 | tf_op jit(solution)/shard_map/ppermute | solution.py:33
  18.2 1.6 fusion.116
  19.8 1.4 broadcast_multiply_fusion.30
  21.3 1.4 broadcast_multiply_fusion.20
  22.7 1.3 broadcast_multiply_fusion.32
  24.0 1.3 broadcast_multiply_fusion.22
  25.3 1.3 broadcast_multiply_fusion.35
  26.6 1.3 broadcast_multiply_fusion.25
  27.9 1.3 broadcast_multiply_fusion.37
  29.1 1.3 broadcast_multiply_fusion.27
  30.4 1.6 fusion.117
  32.0 1.3 add_cosine_fusion.28
  33.3 1.3 add_cosine_fusion.20
  34.6 1.3 add_cosine_fusion.30
  35.9 1.3 add_cosine_fusion.22
  37.2 1.3 add_cosine_fusion.24
  38.6 1.3 add_cosine_fusion.16
  39.9 1.4 add_cosine_fusion.26
  41.3 1.4 add_cosine_fusion.18
  42.9 1.4 broadcast_multiply_fusion.10
  44.4 1.3 broadcast_multiply_fusion.12
  45.7 1.3 broadcast_multiply_fusion.15
  46.9 1.3 broadcast_multiply_fusion.17
  48.2 1.3 add_cosine_fusion.8
  49.6 1.4 add_cosine_fusion.10
  50.9 1.3 add_cosine_fusion.12
  52.2 1.3 add_cosine_fusion.14
  53.8 1.4 broadcast_multiply_fusion
  55.2 1.3 broadcast_multiply_fusion.2
  56.5 1.3 broadcast_multiply_fusion.5
  57.8 1.3 broadcast_multiply_fusion.7
  59.1 1.3 add_cosine_fusion
  60.4 1.4 add_cosine_fusion.2
  62.0 1.3 convert_reduce_fusion
  63.2 1.1 cosine_multiply_fusion
  64.4 1.1 cosine_multiply_fusion.1
  65.5 1.3 add_cosine_fusion.4
  67.0 4.0 %collective-permute-start.2 = (f32[6,144,8]{2,1,0:T(8,128)S(1)}, f32[6,144,8]{2,1,0:T(8,128)S(1)}, u32[]{:S(2)}, u32[]{:S(2)}) collective-permute-start(f32[6,144,8]{2,1,0:T(8,128)S(1)} %get-tuple-element.47), channel_id=1, source_target_pairs={{0,16},{1,17},{2,18},{3,19},{4,20},{5,21},{6,22},{7,23},{8,24},{9,... | collective-permute-start | bytes 82952 | tf_op jit(solution)/shard_map/ppermute | solution.py:31
  71.0 1.3 collective-permute-start.3
  72.3 1.3 add_cosine_fusion.6
  73.7 1.2 dynamic-slice
  75.5 2.2 collective-permute-done.2
  77.7 4.2 %collective-permute-done.3 = f32[6,144,8]{2,1,0:T(8,128)} collective-permute-done((f32[6,144,8]{2,1,0:T(8,128)S(1)}, f32[6,144,8]{2,1,0:T(8,128)}, u32[]{:S(2)}, u32[]{:S(2)}) %collective-permute-start.3) | collective-permute-done | bytes 27680 | tf_op jit(solution)/shard_map/ppermute | solution.py:33
  82.0 1.4 pad_maximum_fusion
  83.9 0.5 slice_subtract_fusion.5
  84.8 0.5 slice_subtract_fusion
  85.6 0.4 slice_subtract_fusion.13
  86.8 0.7 multiply_reduce_fusion
  87.5 39.7 %psum.7 = f32[]{:T(128)} all-reduce(f32[]{:T(128)} %get-tuple-element.4), channel_id=1, replica_groups=mesh['lat'=2,'lon'=16] {'lat','lon'}, use_global_device_ids=true, to_apply=%region_1.2 | all-reduce | flops 1 | bytes 8 | tf_op jit(solution)/shard_map/psum | solution.py:148
  128.5 1.0 fusion.3
  130.0 65.9 %all-reduce.2 = bf16[512,2,128]{2,1,0:T(2,128)(2,1)S(1)} all-reduce(f32[512,2,128]{2,1,0:T(2,128)S(1)} %copy.15), channel_id=3, replica_groups=mesh['lat'=2,'lon'=16] {'lon'}, use_global_device_ids=true, to_apply=%region_3.4.clone | all-reduce | flops 131072 | bytes 786432
  195.8 5.7 %fusion.86 = f32[32,2,1024]{2,1,0:T(2,128)S(1)} fusion(bf16[32,1024,128]{2,1,0:T(8,128)(2,1)} %param.20, bf16[512,2,128]{2,1,0:T(2,128)(2,1)S(1)} %all-reduce.2, u32[]{:T(128)S(6)} %multiply.402), kind=kOutput, calls=%fused_computation.152 | convolution fusion | flops 16777216 | bytes 8667140 | tf_op jit(solution)/shard_map/dot_general | solution.py:164
  201.5 7.0 %all-gather = f32[64,2,1024]{2,1,0:T(2,128)S(1)} all-gather(f32[32,2,1024]{2,1,0:T(2,128)S(1)} %fusion.86), channel_id=2, replica_groups=mesh['lat'=2,'lon'=16] {'lat'}, dimensions={0}, use_global_device_ids=true | all-gather | bytes 786432 | tf_op jit(solution)/shard_map/all_gather | solution.py:18
  209.0 4.6 %fusion.66 = f32[32,2,128]{2,1,0:T(2,128)S(1)} fusion(bf16[32,1024,128]{2,1,0:T(8,128)(2,1)} %param.20, f32[32,2,1024]{2,1,0:T(2,128)S(1)} %reduce_sum.29, f32[1024]{0:T(1024)S(1)} %copy-done.2), kind=kOutput, calls=%fused_computation.122 | convolution fusion | flops 16908288 | bytes 8687616 | tf_op jit(solution)/shard_map/dot_general | solution.py:169
  213.6 2.8 %convolution_bitcast_fusion = f32[2048,128]{1,0:T(8,128)} fusion(f32[2048,32,1]{0,1,2:T(8,128)S(1)} %get-tuple-element.62, f32[2048,32,1]{0,1,2:T(8,128)S(1)} %get-tuple-element.61, f32[32,2,128]{2,1,0:T(2,128)S(1)} %fusion.66), kind=kOutput, calls=%fused_computation | convolution fusion | flops 201457664 | bytes 1605632 | tf_op jit(solution)/shard_map/dot_general | solution.py:179
  216.5 0.8 fusion.74
  217.4 54.8 %reduce-scatter.2.cloned.1.call-done = f32[128,128]{1,0:T(8,128)} async-done(((f32[2048,128]{1,0:T(8,128)}), f32[128,128]{1,0:T(8,128)}) %reduce-scatter.2.cloned.1.call-update) | async-done | bytes 65552 | tf_op jit(solution)/shard_map/reduce_scatter | solution.py:178
  (39 shorter events, 4.2 us)
Async XLA Ops:
  7.2 264.9 %reduce-scatter.2.cloned.1.call-start = ((), (), s32[]{:S(2)}) async-start(), calls=%async_computation.1 | async-start | bytes 1114112 | tf_op jit(solution)/shard_map/reduce_scatter | solution.py:178
  12.3 54.5 %collective-permute-start = (f32[6,8,128]{2,1,0:T(8,128)S(1)}, f32[6,8,128]{2,1,0:T(8,128)S(1)}, u32[]{:S(2)}, u32[]{:S(2)}) collective-permute-start(f32[6,8,128]{2,1,0:T(8,128)S(1)} %get-tuple-element.49), channel_id=1, source_target_pairs={{0,1},{1,2},{2,3},{3,4},{4,5},{5,6},{6,7},{7,8},{8,9},{9,10},{10,1... | collective-permute-start | bytes 73736 | tf_op jit(solution)/shard_map/ppermute | solution.py:31
  12.8 53.9 %collective-permute-start.1 = (f32[6,8,128]{2,1,0:T(8,128)S(1)}, f32[6,8,128]{2,1,0:T(8,128)S(1)}, u32[]{:S(2)}, u32[]{:S(2)}) collective-permute-start(f32[6,8,128]{2,1,0:T(8,128)S(1)} %get-tuple-element.50), channel_id=1, source_target_pairs={{1,0},{2,1},{3,2},{4,3},{5,4},{6,5},{7,6},{8,7},{9,8},{10,9},{11,1... | collective-permute-start | bytes 73736 | tf_op jit(solution)/shard_map/ppermute | solution.py:33
  67.0 19.8 %copy-start = (s32[128,128]{1,0:T(8,128)S(1)}, s32[128,128]{1,0:T(8,128)}, u32[]{:S(2)}) copy-start(s32[128,128]{1,0:T(8,128)} %param.15) | copy-start | bytes 196612
  67.0 10.7 %collective-permute-start.2 = (f32[6,144,8]{2,1,0:T(8,128)S(1)}, f32[6,144,8]{2,1,0:T(8,128)S(1)}, u32[]{:S(2)}, u32[]{:S(2)}) collective-permute-start(f32[6,144,8]{2,1,0:T(8,128)S(1)} %get-tuple-element.47), channel_id=1, source_target_pairs={{0,16},{1,17},{2,18},{3,19},{4,20},{5,21},{6,22},{7,23},{8,24},{9,... | collective-permute-start | bytes 82952 | tf_op jit(solution)/shard_map/ppermute | solution.py:31
  71.0 11.0 %collective-permute-start.3 = (f32[6,144,8]{2,1,0:T(8,128)S(1)}, f32[6,144,8]{2,1,0:T(8,128)}, u32[]{:S(2)}, u32[]{:S(2)}) collective-permute-start(f32[6,144,8]{2,1,0:T(8,128)S(1)} %get-tuple-element.48), channel_id=1, source_target_pairs={{16,0},{17,1},{18,2},{19,3},{20,4},{21,5},{22,6},{23,7},{24,8},{25... | collective-permute-start | bytes 82952 | tf_op jit(solution)/shard_map/ppermute | solution.py:33
  86.0 123.0 %copy-start.2 = (f32[1024]{0:T(1024)S(1)}, f32[1024]{0:T(1024)}, u32[]{:S(2)}) copy-start(f32[1024]{0:T(1024)} %param.21) | copy-start | bytes 12292
  87.5 126.1 %copy-start.1 = (f32[128,128]{1,0:T(8,128)}, f32[128,128]{1,0:T(8,128)S(1)}, u32[]{:S(2)}) copy-start(f32[128,128]{1,0:T(8,128)S(1)} %get-tuple-element.5) | copy-start | bytes 196612
Sparse Core Ops, SparseCore 0:
  216.5 55.5 reduce-scatter.1
